TPU v7x, 256 devices: a whole 4x4x8 slice. The times are simulated.
256 devices in a mesh: imp: 32 (over z, y_hi, core), cre: 8 (over x, y_lo).
Axes of the slice: x: 4, y: 4 (y_hi: 2, y_lo: 2; y = y_hi * 2 + y_lo), z: 8, core: 2. Of those that a mesh axis runs over, the one named last changes fastest.
Arguments:
- impressions: bfloat16 [32768, 256], P('imp'), may hold values from -24 to 24
- panels: bfloat16 [8, 2048, 256], P('cre', 'imp'), may hold values from -2 to 2
- block_lists: int32 [256, 16], P('imp'), may hold values from 0 to 127, as said below
- block_counts: int32 [256], P('imp'), may hold values from 1 to 16, as said below
- imp_weight: float32 [32768], P('imp'), may hold values from 0.2 to 5
- spend_goals: float32 [8, 2048], P('cre', 'imp'), may hold values from 0.2 to 5
- prices: float32 [8, 2048], P('cre', 'imp'), may hold values from -1 to 1
Outputs:
- final_prices: float32 [8, 2048], P('cre', 'imp')
- final_spend: float32 [8, 2048], P('cre', 'imp')
- log_norm: float32 [32768], P('imp')
Inputs may be any that keep to these rules, and one draw needn't show every extreme that they name: `block_lists`: each row lists 16 different block ids; only the first block_counts entries of a row are eligible for the 128 impressions of that tile, the others must be ignored. `block_counts`: some tile has 16 eligible blocks.
All inputs are finite; a program needn't handle non-finite values.
Results may differ from a plain program's by a relative error of at most 0.0003.
Values may be sent and summed in bfloat16 or wider, within the bound.
A program may use at most 64 MiB of HBM per device.

v0:
```python
import jax
import jax.numpy as jnp
from jax import lax
from jax.sharding import PartitionSpec as P

CRE_LOC = 2048
TILE = 128
BLOCK = 128
ITERS = 2
NEG_FILL = -1e30
TAU_INV = 4.0
STEP_RATE = 0.5


def block_table(block_lists, block_counts, local_blocks, cre_index):
    block_ids = cre_index * local_blocks + lax.iota(jnp.int32, local_blocks)
    in_list = lax.iota(jnp.int32, block_lists.shape[1])[None, :] < block_counts[:, None]
    matches = (block_lists[:, :, None] == block_ids[None, None, :]) & in_list[:, :, None]
    allowed = jnp.any(matches, axis=1)
    allowed = jnp.repeat(allowed, TILE, axis=0)
    return jnp.repeat(allowed, BLOCK, axis=1)


def scored(impressions, panel_rows, price_rows, col_mask):
    affinity = lax.dot_general(
        impressions, panel_rows, (((1,), (1,)), ((), ())), preferred_element_type=jnp.float32
    )
    logit_vals = TAU_INV * affinity + price_rows[None, :]
    return jnp.where(col_mask, logit_vals, NEG_FILL)


def sweep(panel_rows, group_prices, mask_full, running, update):
    col_count = panel_rows.shape[0]
    sub_width = 512

    def inner(current, step_index):
        shift_cols = step_index * sub_width
        part_panel = lax.dynamic_slice_in_dim(panel_rows, shift_cols, sub_width, 0)
        part_price = lax.dynamic_slice_in_dim(group_prices, shift_cols, sub_width, 0)
        part_mask = lax.dynamic_slice_in_dim(mask_full, shift_cols, sub_width, 1)
        return (update(current, part_panel, part_price, part_mask, shift_cols), None)

    current, _ = lax.scan(inner, running, jnp.arange(col_count // sub_width, dtype=jnp.int32))
    return current


def shards(impressions, panels, block_lists, block_counts, imp_weight, spend_goals, prices):
    local_blocks = CRE_LOC // BLOCK
    mask_full = block_table(block_lists, block_counts, local_blocks, lax.axis_index("cre"))
    imp_rows = impressions.shape[0]
    owned_rows = prices.shape[1]
    owned_start = lax.axis_index("imp") * owned_rows

    def max_step(current, panel_rows, price_rows, col_mask, first_col):
        row_top, row_total = current
        masked = scored(impressions, panel_rows, price_rows, col_mask)
        block_top = jnp.max(masked, axis=1)
        new_top = jnp.maximum(row_top, block_top)
        block_sum = jnp.sum(jnp.where(col_mask, jnp.exp(masked - block_top[:, None]), 0.0), axis=1)
        return (
            new_top,
            row_total * jnp.exp(row_top - new_top) + block_sum * jnp.exp(block_top - new_top),
        )

    spend_owned = None
    row_norm = None
    for iteration in range(ITERS):
        start_state = (
            jnp.full((imp_rows,), NEG_FILL, jnp.float32),
            jnp.zeros((imp_rows,), jnp.float32),
        )
        empty_spend = jnp.zeros((CRE_LOC,), jnp.float32)
        whole_prices = lax.all_gather(prices, "imp", axis=1, tiled=True)[0]
        row_top, row_total = sweep(
            lax.all_gather(panels, "imp", axis=1, tiled=True)[0],
            whole_prices,
            mask_full,
            start_state,
            max_step,
        )
        merged_top = lax.pmax(row_top, "cre")
        row_total = lax.psum(row_total * jnp.exp(row_top - merged_top), "cre")
        row_top = merged_top
        row_norm = row_top + jnp.log(row_total)

        def spend_step(current, panel_rows, price_rows, col_mask, first_col):
            masked = scored(impressions, panel_rows, price_rows, col_mask)
            shares = jnp.where(col_mask, jnp.exp(masked - row_norm[:, None]), 0.0)
            col_spend = jnp.sum(imp_weight[:, None] * shares, axis=0)
            return lax.dynamic_update_slice_in_dim(current, col_spend, first_col, 0)

        partial_spend = sweep(
            lax.all_gather(panels, "imp", axis=1, tiled=True)[0],
            whole_prices,
            mask_full,
            empty_spend,
            spend_step,
        )
        summed = lax.psum(partial_spend, "imp")
        spend_owned = lax.dynamic_slice_in_dim(summed, owned_start, owned_rows, 0)
        spend_owned = spend_owned.reshape(1, owned_rows)
        prices = prices + STEP_RATE * (
            jnp.log(spend_goals) - jnp.log(spend_owned + 0.25 * spend_goals)
        )
    return (prices, spend_owned, row_norm)


def solution(mesh):
    placed = (
        P("imp", None),
        P("cre", "imp", None),
        P("imp", None),
        P("imp"),
        P("imp"),
        P("cre", "imp"),
        P("cre", "imp"),
    )
    return jax.shard_map(
        shards,
        mesh=mesh,
        in_specs=placed,
        out_specs=(P("cre", "imp"), P("cre", "imp"), P("imp")),
        check_vma=False,
    )
```

profile of v0, /device:TPU:1, one launch (start us, length us, event | category | flops | bytes accessed | tf_op | source)
XLA Modules:
  0.0 427.9 jit_solution(15510092804575440473)
XLA Ops:
  8.7 0.8 and_reduce_fusion
  9.7 1.3 dynamic-slice
  11.6 0.8 bitcast_dynamic-update-slice_fusion.1
  12.4 70.3 %all-reduce = f32[2048]{0:T(1024)S(1)} all-reduce(f32[2048]{0:T(1024)S(1)} %bitcast_dynamic-update-slice_fusion.1), channel_id=1, replica_groups=mesh['imp'=32,'cre'=8] {'imp'}, use_global_device_ids=true, to_apply=%add | all-reduce | flops 2048 | bytes 16384 | tf_op jit(solution)/shard_map/squeeze | solution.py:73
  82.8 9.8 %all-gather.2.cloned.1.call-done = bf16[1,2048,256]{2,1,0:T(8,128)(2,1)} async-done(((bf16[1,64,256]{2,1,0:T(8,128)(2,1)}), bf16[1,2048,256]{2,1,0:T(8,128)(2,1)}) %all-gather.2.cloned.1.call-update) | async-done | bytes 1048592 | tf_op jit(solution)/shard_map/all_gather | solution.py:93
  93.7 15.7 %while.48 = (s32[]{:T(128)}, f32[1024]{0:T(1024)S(1)}, f32[1024]{0:T(1024)S(1)}, s32[4]{0:T(128)S(1)}, pred[1024,2048]{0,1:T(32,128)(4,1)S(1)}, /*index=5*/bf16[...) while((s32[]{:T(128)}, f32[1024]{0:T(1024)S(1)}, ...), condition=%wide.region_4.5_spmd.clone, body=%wide.region_1.4_spmd.clone.sunk | while | flops 273684480 | bytes 6075585 | solution.py:43
  95.2 1.7 fusion.49
  99.1 1.7 fusion.49
  103.0 1.7 fusion.49
  107.0 1.7 fusion.49
  109.4 14.9 %pmax.14 = f32[1024]{0:T(1024)S(1)} all-reduce(f32[1024]{0:T(1024)S(1)} %get-tuple-element.183), channel_id=1, replica_groups=mesh['imp'=32,'cre'=8] {'cre'}, use_global_device_ids=true, to_apply=%region_5.6 | all-reduce | flops 1024 | bytes 8192 | tf_op jit(solution)/shard_map/pmax | solution.py:81
  124.4 12.5 %psum.28 = f32[1024]{0:T(1024)S(1)} all-reduce(f32[1024]{0:T(1024)S(1)} %exponential_multiply_fusion.1), channel_id=1, replica_groups=mesh['imp'=32,'cre'=8] {'cre'}, use_global_device_ids=true, to_apply=%region_6.7 | all-reduce | flops 1024 | bytes 8192 | tf_op jit(solution)/shard_map/psum | solution.py:82
  136.9 14.6 %while.46 = (s32[]{:T(128)}, f32[2048]{0:T(1024)S(1)}, f32[1024]{0:T(1024)S(1)}, s32[4]{0:T(128)S(1)}, pred[1024,2048]{0,1:T(32,128)(4,1)S(1)}, /*index=5*/bf16[...) while((s32[]{:T(128)}, f32[2048]{0:T(1024)S(1)}, ...), condition=%wide.region_9.10_spmd, body=%wide.region_7.9_spmd.sunk | while | flops 272104960 | bytes 1332415 | solution.py:43
  138.2 2.1 fusion.44
  141.9 2.1 fusion.44
  145.6 2.1 fusion.44
  149.2 2.1 fusion.44
  151.5 72.9 %psum.29 = f32[2048]{0:T(1024)S(1)} all-reduce(f32[2048]{0:T(1024)S(1)} %get-tuple-element.185), channel_id=1, replica_groups=mesh['imp'=32,'cre'=8] {'imp'}, use_global_device_ids=true, to_apply=%region_10.11 | all-reduce | flops 2048 | bytes 16384 | tf_op jit(solution)/shard_map/psum | solution.py:99
  224.6 66.0 %all-reduce.1 = f32[2048]{0:T(1024)S(1)} all-reduce(f32[2048]{0:T(1024)S(1)} %get-tuple-element.317), channel_id=1, replica_groups=mesh['imp'=32,'cre'=8] {'imp'}, use_global_device_ids=true, to_apply=%add.1 | all-reduce | flops 2048 | bytes 16384 | tf_op jit(solution)/shard_map/squeeze | solution.py:73
  290.7 15.2 %while.49 = (s32[]{:T(128)}, f32[1024]{0:T(1024)S(1)}, f32[1024]{0:T(1024)S(1)}, s32[4]{0:T(128)S(1)}, pred[1024,2048]{0,1:T(32,128)(4,1)S(1)}, /*index=5*/bf16[...) while((s32[]{:T(128)}, f32[1024]{0:T(1024)S(1)}, ...), condition=%wide.region_14.15_spmd.clone, body=%wide.region_11.14_spmd.clone.sunk | while | flops 273684480 | bytes 6075585 | solution.py:43
  292.0 1.7 fusion.52
  295.8 1.7 fusion.52
  299.6 1.7 fusion.52
  303.4 1.7 fusion.52
  305.9 14.2 %pmax.15 = f32[1024]{0:T(1024)S(1)} all-reduce(f32[1024]{0:T(1024)S(1)} %get-tuple-element.186), channel_id=1, replica_groups=mesh['imp'=32,'cre'=8] {'cre'}, use_global_device_ids=true, to_apply=%region_15.16 | all-reduce | flops 1024 | bytes 8192 | tf_op jit(solution)/shard_map/pmax | solution.py:81
  320.0 12.8 %psum.30 = f32[1024]{0:T(1024)S(1)} all-reduce(f32[1024]{0:T(1024)S(1)} %exponential_multiply_fusion), channel_id=1, replica_groups=mesh['imp'=32,'cre'=8] {'cre'}, use_global_device_ids=true, to_apply=%region_16.17 | all-reduce | flops 1024 | bytes 8192 | tf_op jit(solution)/shard_map/psum | solution.py:82
  332.8 14.6 %while.47 = (s32[]{:T(128)}, f32[2048]{0:T(1024)S(1)}, f32[1024]{0:T(1024)S(1)}, s32[4]{0:T(128)S(1)}, pred[1024,2048]{0,1:T(32,128)(4,1)S(1)}, /*index=5*/bf16[...) while((s32[]{:T(128)}, f32[2048]{0:T(1024)S(1)}, ...), condition=%wide.region_19.20_spmd, body=%wide.region_17.19_spmd.sunk | while | flops 272104960 | bytes 1332415 | solution.py:43
  334.1 2.1 fusion.47
  337.8 2.1 fusion.47
  341.5 2.1 fusion.47
  345.1 2.1 fusion.47
  347.4 73.0 %psum.31 = f32[2048]{0:T(1024)S(1)} all-reduce(f32[2048]{0:T(1024)S(1)} %get-tuple-element.188), channel_id=1, replica_groups=mesh['imp'=32,'cre'=8] {'imp'}, use_global_device_ids=true, to_apply=%region_20.21 | all-reduce | flops 2048 | bytes 16384 | tf_op jit(solution)/shard_map/psum | solution.py:99
  (92 shorter events, 23.0 us)
Async XLA Ops:
  7.2 85.4 %all-gather.2.cloned.1.call-start = ((), (), s32[]{:S(2)}) async-start(), calls=%async_computation | async-start | bytes 1081344 | tf_op jit(solution)/shard_map/all_gather | solution.py:93
  92.5 1.2 copy-start.3
  93.7 43.1 %copy-start.4 = (f32[1024]{0:T(1024)S(1)}, f32[1024]{0:T(1024)}, u32[]{:S(2)}) copy-start(f32[1024]{0:T(1024)} %param.19) | copy-start | bytes 12292
  136.9 87.5 %copy-start.1 = (f32[1,64]{1,0:T(1,128)S(1)}, f32[1,64]{1,0:T(1,128)}, u32[]{:S(2)}) copy-start(f32[1,64]{1,0:T(1,128)} %param.20) | copy-start | bytes 772
  136.9 87.5 %copy-start.2 = (f32[1,64]{1,0:T(1,128)S(1)}, f32[1,64]{1,0:T(1,128)}, u32[]{:S(2)}) copy-start(f32[1,64]{1,0:T(1,128)} %param.21) | copy-start | bytes 772
  347.4 73.7 %copy-start = (f32[1024]{0:T(1024)}, f32[1024]{0:T(1024)S(1)}, u32[]{:S(2)}) copy-start(f32[1024]{0:T(1024)S(1)} %get-tuple-element.705) | copy-start | bytes 12292
Sparse Core Ops, SparseCore 0:
  10.8 81.6 all-gather.1
where the time goes:
time: 429 us; the launch traced here: 428 us
  blocking collectives  337 us (79%)
  matrix products  29.8 us (7%)
  local copies, waits for them, and re-layouts  16.5 us (4%)
  between operations  14.9 us (3%)
  loops' own time  11 us (3%)
  waiting for transfers between devices  10.4 us (2%)
  other arithmetic  8.58 us (2%)
    psum x2, blocking collectives, shards(): summed = lax.psum(partial_spend, 'imp')  146 us
    squeeze x2, blocking collectives, shards(): whole_prices = lax.all_gather(prices, 'imp', axis=1, tiled=True)[0]  136 us
    dot_general x16, matrix products, scored(): lax.dot_general(impressions, panel_rows, (((1,), (1,)), ((), ())), prefer...  29.8 us
    pmax x2, blocking collectives, shards(): merged_top = lax.pmax(row_top, 'cre')  29.1 us
    psum x2, blocking collectives, shards(): row_total = lax.psum(row_total * jnp.exp(row_top - merged_top), 'cre')  25.2 us
    another operation x4, loops' own time, sweep(): lax.scan(inner, running, jnp.arange(col_count // sub_width, dtype=jnp.int...  11 us
    all_gather x1, waiting for transfers between devices, shards(): lax.all_gather(panels, 'imp', axis=1, tiled=True)[0]  9.76 us
    dynamic_slice x16, local copies, waits for them, and re-layouts, sweep(): lax.scan(inner, running, jnp.arange(col_count // sub_width, dtype=jnp.int...  9.67 us
  transfers between devices with their start and end apart: 1, of which 1 were waited for; matrix products, arithmetic and copies ran while one was open for 1% of the time, Pallas kernels for 0%

commit v1 on v0

--- a/solution.py
+++ b/solution.py
@@ -10,6 +10,11 @@
 NEG_FILL = -1e30
 TAU_INV = 4.0
 STEP_RATE = 0.5
+
+
+def summed_here(array, axis):
+    shards = lax.all_gather(array, axis)
+    return jnp.sum(shards, axis=0)
 
 
 def block_table(block_lists, block_counts, local_blocks, cre_index):
@@ -79,7 +84,7 @@
             max_step,
         )
         merged_top = lax.pmax(row_top, "cre")
-        row_total = lax.psum(row_total * jnp.exp(row_top - merged_top), "cre")
+        row_total = summed_here(row_total * jnp.exp(row_top - merged_top), "cre")
         row_top = merged_top
         row_norm = row_top + jnp.log(row_total)
 

time: 429 us -> 451 us (1.051)
  blocking collectives: 337 us -> 359 us
    all_gather x0 -> x2, blocking collectives: none -> 43.4 us  [summed_here(): shards = lax.all_gather(array, axis)]
    psum x2 -> x0, blocking collectives: 25.2 us -> none  [shards(): row_total = lax.psum(row_total * jnp.exp(row_top - merged_top), 'cre')]
    psum x2, blocking collectives: 146 us -> 152 us  [shards(): summed = lax.psum(partial_spend, 'imp')]
where the time goes in v1:
time: 451 us; the launch traced here: 450 us
  blocking collectives  359 us (80%)
  matrix products  29.8 us (7%)
  local copies, waits for them, and re-layouts  16.5 us (4%)
  between operations  14.9 us (3%)
  loops' own time  11 us (2%)
  waiting for transfers between devices  10.4 us (2%)
  other arithmetic  8.59 us (2%)
    psum x2, blocking collectives, shards(): summed = lax.psum(partial_spend, 'imp')  152 us
    squeeze x2, blocking collectives, shards(): whole_prices = lax.all_gather(prices, 'imp', axis=1, tiled=True)[0]  136 us
    all_gather x2, blocking collectives, summed_here(): shards = lax.all_gather(array, axis)  43.4 us
    dot_general x16, matrix products, scored(): lax.dot_general(impressions, panel_rows, (((1,), (1,)), ((), ())), prefer...  29.8 us
    pmax x2, blocking collectives, shards(): merged_top = lax.pmax(row_top, 'cre')  27.4 us
    another operation x4, loops' own time, sweep(): lax.scan(inner, running, jnp.arange(col_count // sub_width, dtype=jnp.int...  11 us
    all_gather x1, waiting for transfers between devices, shards(): lax.all_gather(panels, 'imp', axis=1, tiled=True)[0]  9.76 us
    dynamic_slice x16, local copies, waits for them, and re-layouts, sweep(): lax.scan(inner, running, jnp.arange(col_count // sub_width, dtype=jnp.int...  9.67 us
  transfers between devices with their start and end apart: 1, of which 1 were waited for; matrix products, arithmetic and copies ran while one was open for 1% of the time, Pallas kernels for 0%

profile of v1, /device:TPU:1, one launch (start us, length us, event | category | flops | bytes accessed | tf_op | source)
XLA Modules:
  0.0 450.2 jit_solution(1288529005281568920)
XLA Ops:
  8.7 0.8 and_reduce_fusion
  9.7 1.3 dynamic-slice
  11.6 0.8 bitcast_dynamic-update-slice_fusion.1
  12.4 70.3 %all-reduce = f32[2048]{0:T(1024)S(1)} all-reduce(f32[2048]{0:T(1024)S(1)} %bitcast_dynamic-update-slice_fusion.1), channel_id=1, replica_groups=mesh['imp'=32,'cre'=8] {'imp'}, use_global_device_ids=true, to_apply=%add | all-reduce | flops 2048 | bytes 16384 | tf_op jit(solution)/shard_map/squeeze | solution.py:78
  82.8 9.8 %all-gather.4.cloned.1.call-done = bf16[1,2048,256]{2,1,0:T(8,128)(2,1)} async-done(((bf16[1,64,256]{2,1,0:T(8,128)(2,1)}), bf16[1,2048,256]{2,1,0:T(8,128)(2,1)}) %all-gather.4.cloned.1.call-update) | async-done | bytes 1048592 | tf_op jit(solution)/shard_map/all_gather | solution.py:98
  93.7 15.7 %while.48 = (s32[]{:T(128)}, f32[1024]{0:T(1024)S(1)}, f32[1024]{0:T(1024)S(1)}, s32[4]{0:T(128)S(1)}, pred[1024,2048]{0,1:T(32,128)(4,1)S(1)}, /*index=5*/bf16[...) while((s32[]{:T(128)}, f32[1024]{0:T(1024)S(1)}, ...), condition=%wide.region_4.5_spmd.clone, body=%wide.region_1.4_spmd.clone.sunk | while | flops 273684480 | bytes 6075585 | solution.py:48
  95.2 1.7 fusion.49
  99.1 1.7 fusion.49
  103.0 1.7 fusion.49
  106.9 1.7 fusion.49
  109.4 14.9 %pmax.14 = f32[1024]{0:T(1024)S(1)} all-reduce(f32[1024]{0:T(1024)S(1)} %get-tuple-element.183), channel_id=1, replica_groups=mesh['imp'=32,'cre'=8] {'cre'}, use_global_device_ids=true, to_apply=%region_5.6 | all-reduce | flops 1024 | bytes 8192 | tf_op jit(solution)/shard_map/pmax | solution.py:86
  124.3 21.7 %all-gather = f32[8192]{0:T(1024)S(1)} all-gather(f32[1024]{0:T(1024)S(1)} %exponential_multiply_fusion.1), channel_id=2, replica_groups=mesh['imp'=32,'cre'=8] {'cre'}, dimensions={0}, use_global_device_ids=true | all-gather | bytes 36864 | tf_op jit(solution)/shard_map/all_gather | solution.py:16
  146.1 14.6 %while.46 = (s32[]{:T(128)}, f32[2048]{0:T(1024)S(1)}, f32[1024]{0:T(1024)S(1)}, s32[4]{0:T(128)S(1)}, pred[1024,2048]{0,1:T(32,128)(4,1)S(1)}, /*index=5*/bf16[...) while((s32[]{:T(128)}, f32[2048]{0:T(1024)S(1)}, ...), condition=%wide.region_9.10_spmd, body=%wide.region_7.9_spmd.sunk | while | flops 272104960 | bytes 1332415 | solution.py:48
  147.5 2.1 fusion.44
  151.1 2.1 fusion.44
  154.8 2.1 fusion.44
  158.4 2.1 fusion.44
  160.8 75.7 %psum.14 = f32[2048]{0:T(1024)S(1)} all-reduce(f32[2048]{0:T(1024)S(1)} %get-tuple-element.185), channel_id=1, replica_groups=mesh['imp'=32,'cre'=8] {'imp'}, use_global_device_ids=true, to_apply=%region_10.11 | all-reduce | flops 2048 | bytes 16384 | tf_op jit(solution)/shard_map/psum | solution.py:104
  236.7 66.0 %all-reduce.1 = f32[2048]{0:T(1024)S(1)} all-reduce(f32[2048]{0:T(1024)S(1)} %get-tuple-element.317), channel_id=1, replica_groups=mesh['imp'=32,'cre'=8] {'imp'}, use_global_device_ids=true, to_apply=%add.1 | all-reduce | flops 2048 | bytes 16384 | tf_op jit(solution)/shard_map/squeeze | solution.py:78
  302.8 15.2 %while.49 = (s32[]{:T(128)}, f32[1024]{0:T(1024)S(1)}, f32[1024]{0:T(1024)S(1)}, s32[4]{0:T(128)S(1)}, pred[1024,2048]{0,1:T(32,128)(4,1)S(1)}, /*index=5*/bf16[...) while((s32[]{:T(128)}, f32[1024]{0:T(1024)S(1)}, ...), condition=%wide.region_14.15_spmd.clone, body=%wide.region_11.14_spmd.clone.sunk | while | flops 273684480 | bytes 6075585 | solution.py:48
  304.1 1.7 fusion.52
  307.9 1.7 fusion.52
  311.7 1.7 fusion.52
  315.5 1.7 fusion.52
  318.0 12.5 %pmax.15 = f32[1024]{0:T(1024)S(1)} all-reduce(f32[1024]{0:T(1024)S(1)} %get-tuple-element.186), channel_id=1, replica_groups=mesh['imp'=32,'cre'=8] {'cre'}, use_global_device_ids=true, to_apply=%region_15.16 | all-reduce | flops 1024 | bytes 8192 | tf_op jit(solution)/shard_map/pmax | solution.py:86
  330.5 21.7 %all-gather.1 = f32[8192]{0:T(1024)S(1)} all-gather(f32[1024]{0:T(1024)S(1)} %exponential_multiply_fusion), channel_id=3, replica_groups=mesh['imp'=32,'cre'=8] {'cre'}, dimensions={0}, use_global_device_ids=true | all-gather | bytes 36864 | tf_op jit(solution)/shard_map/all_gather | solution.py:16
  352.2 14.6 %while.47 = (s32[]{:T(128)}, f32[2048]{0:T(1024)S(1)}, f32[1024]{0:T(1024)S(1)}, s32[4]{0:T(128)S(1)}, pred[1024,2048]{0,1:T(32,128)(4,1)S(1)}, /*index=5*/bf16[...) while((s32[]{:T(128)}, f32[2048]{0:T(1024)S(1)}, ...), condition=%wide.region_19.20_spmd, body=%wide.region_17.19_spmd.sunk | while | flops 272104960 | bytes 1332415 | solution.py:48
  353.6 2.1 fusion.47
  357.2 2.1 fusion.47
  360.9 2.1 fusion.47
  364.5 2.1 fusion.47
  366.8 75.9 %psum.15 = f32[2048]{0:T(1024)S(1)} all-reduce(f32[2048]{0:T(1024)S(1)} %get-tuple-element.188), channel_id=1, replica_groups=mesh['imp'=32,'cre'=8] {'imp'}, use_global_device_ids=true, to_apply=%region_20.21 | all-reduce | flops 2048 | bytes 16384 | tf_op jit(solution)/shard_map/psum | solution.py:104
  (96 shorter events, 23.0 us)
Async XLA Ops:
  7.2 85.4 %all-gather.4.cloned.1.call-start = ((), (), s32[]{:S(2)}) async-start(), calls=%async_computation | async-start | bytes 1081344 | tf_op jit(solution)/shard_map/all_gather | solution.py:98
  92.5 1.2 copy-start.3
  93.7 52.4 %copy-start.4 = (f32[1024]{0:T(1024)S(1)}, f32[1024]{0:T(1024)}, u32[]{:S(2)}) copy-start(f32[1024]{0:T(1024)} %param.19) | copy-start | bytes 12292
  146.1 90.4 %copy-start.1 = (f32[1,64]{1,0:T(1,128)S(1)}, f32[1,64]{1,0:T(1,128)}, u32[]{:S(2)}) copy-start(f32[1,64]{1,0:T(1,128)} %param.20) | copy-start | bytes 772
  146.1 90.4 %copy-start.2 = (f32[1,64]{1,0:T(1,128)S(1)}, f32[1,64]{1,0:T(1,128)}, u32[]{:S(2)}) copy-start(f32[1,64]{1,0:T(1,128)} %param.21) | copy-start | bytes 772
  366.8 76.5 %copy-start = (f32[1024]{0:T(1024)}, f32[1024]{0:T(1024)S(1)}, u32[]{:S(2)}) copy-start(f32[1024]{0:T(1024)S(1)} %get-tuple-element.705) | copy-start | bytes 12292
Sparse Core Ops, SparseCore 0:
  10.8 81.6 all-gather.3
